TPU v7x, 256 devices: a whole 4x4x8 slice. The times are simulated.
256 devices in a mesh: dp: 2 (over core), width: 4 (over x), vocab: 32 (over z, y).
Axes of the slice: x: 4, y: 4, z: 8, core: 2. Of those that a mesh axis runs over, the one named last changes fastest.
Arguments:
- hidden: bfloat16 [1024, 8192], P('dp', 'width'), may hold values from -68 to 68
- head: bfloat16 [8192, 2, 32064], P('width', 'dp', 'vocab'), may hold values from -0.25 to 0.25
- teacher: bfloat16 [1024, 2, 32064], P('dp', None, 'vocab'), may hold values from -180 to 180
Outputs:
- divergence: float32 [1024], P('dp')
- grad_head: bfloat16 [8192, 2, 32064], P('width', 'dp', 'vocab')
- grad_hidden: bfloat16 [1024, 8192], P('dp', 'width')
All inputs are finite; a program needn't handle non-finite values.
Results may differ from a plain program's by a relative error of at most 0.0052.
Values may be sent and summed in bfloat16 or wider, within the bound.
A program may use at most 128 MiB of HBM per device.

v0:
```python
import jax
import jax.numpy as jnp
from jax import lax
from jax.sharding import PartitionSpec as P

VOCAB = 64128


def body(hidden, head, teacher):
    tok_rows, width_cols = hidden.shape
    halves = teacher.shape[1]
    local_cols = teacher.shape[2]
    full_head = lax.all_gather(head, "dp", axis=1, tiled=True).reshape(
        width_cols, halves * local_cols
    )
    partial_value = jnp.dot(hidden, full_head, preferred_element_type=jnp.float32)
    student = lax.psum(partial_value, "width")
    target = teacher.reshape(tok_rows, halves * local_cols).astype(jnp.float32)
    student_peak = jnp.max(student, axis=1)
    target_peak = jnp.max(target, axis=1)
    student_peak, target_peak = lax.pmax((student_peak, target_peak), "vocab")
    target_exp = jnp.exp(target - target_peak[:, None])
    student_total, target_total, cross_total = lax.psum(
        (
            jnp.sum(jnp.exp(student - student_peak[:, None]), axis=1),
            jnp.sum(target_exp, axis=1),
            jnp.sum(target_exp * (target - student), axis=1),
        ),
        "vocab",
    )
    student_lse = student_peak + jnp.log(student_total)
    target_lse = target_peak + jnp.log(target_total)
    divergence = cross_total / target_total - target_lse + student_lse
    prob_student = jnp.exp(student - student_lse[:, None])
    prob_target = jnp.exp(target - target_lse[:, None])
    grad = (VOCAB * (prob_student - prob_target)).astype(jnp.bfloat16)
    grad_blocks = grad.reshape(tok_rows, halves, local_cols)
    blocks = width_cols * lax.axis_size("dp") // width_cols
    term = jnp.einsum("td,tkv->kdv", hidden, grad_blocks, preferred_element_type=jnp.float32)
    head_term = lax.psum_scatter(
        term.reshape(blocks * width_cols, local_cols), "dp", scatter_dimension=0, tiled=True
    )
    grad_head = head_term.astype(jnp.bfloat16).reshape(width_cols, 1, local_cols)
    hidden_term = lax.dot_general(
        grad, full_head, (((1,), (1,)), ((), ())), preferred_element_type=jnp.float32
    )
    grad_hidden = lax.psum(hidden_term, "vocab").astype(jnp.bfloat16)
    return (divergence, grad_head, grad_hidden)


def solution(mesh):
    return jax.shard_map(
        body,
        mesh=mesh,
        in_specs=(P("dp", "width"), P("width", "dp", "vocab"), P("dp", None, "vocab")),
        out_specs=(P("dp"), P("width", "dp", "vocab"), P("dp", "width")),
        check_vma=False,
    )
```

profile of v0, /device:TPU:2, one launch (start us, length us, event | category | flops | bytes accessed | tf_op | source)
XLA Modules:
  0.0 548.4 jit_solution(12567613389792812008)
XLA Ops:
  7.2 0.0 copy-start
  7.2 0.0 all-gather.2.cloned.1.call-start
  7.2 0.7 all-gather.2.cloned.1.call-update
  7.9 0.0 all-reduce.6.cloned.1.call-start
  8.0 29.8 %all-gather.2.cloned.1.call-done = bf16[2048,2,1002]{0,2,1:T(8,128)(2,1)} async-done(((bf16[2048,1,1002]{0,2,1:T(8,128)(2,1)}), bf16[2048,2,1002]{0,2,1:T(8,128)(2,1)}) %all-gather.2.cloned.1.call-update) | async-done | bytes 8208400 | tf_op jit(solution)/shard_map/all_gather | solution.py:13
  37.8 8.1 %reshape.29 = bf16[2048,2004]{0,1:T(8,128)(2,1)} reshape(bf16[2048,2,1002]{0,2,1:T(8,128)(2,1)} %all-gather.2.cloned.1.call-done) | data formatting | bytes 16416768 | tf_op jit(solution)/shard_map/reshape | solution.py:13
  45.9 0.0 copy-done
  45.9 8.8 %fusion.1 = f32[512,2004]{0,1:T(8,128)} fusion(bf16[512,2048]{1,0:T(8,128)(2,1)S(1)} %copy-done, bf16[2048,2004]{0,1:T(8,128)(2,1)} %reshape.29), kind=kOutput, calls=%fused_computation.10 | convolution fusion | flops 4202692608 | bytes 14409728 | tf_op jit(solution)/shard_map/dot_general | solution.py:16
  54.7 0.0 all-reduce.6.cloned.1.call-update
  54.7 0.0 reduce-scatter.2.cloned.1.call-start
  54.7 4.2 copy.13
  58.9 3.3 reduce_max.23
  62.2 4.5 reshape.33
  66.7 84.9 %all-reduce.6.cloned.1.call-done = f32[512,2004]{0,1:T(8,128)} async-done(((f32[512,2004]{0,1:T(8,128)}), f32[512,2004]{0,1:T(8,128)}) %all-reduce.6.cloned.1.call-update) | async-done | bytes 4104208 | tf_op jit(solution)/shard_map/psum | solution.py:17
  151.7 2.5 reduce_max.25
  154.2 75.3 %all-reduce.2 = (f32[512]{0:T(512)S(1)}, f32[512]{0:T(512)S(1)}) all-reduce(f32[512]{0:T(512)S(1)} %reduce_max.25, bf16[512]{0:T(512)(128)(2,1)S(1)} %reduce_max.23), channel_id=1, replica_groups=mesh['dp'=2,'width'=4,'vocab'=32] {'vocab'}, use_global_device_ids=true, to_apply=%region_8.0 | all-reduce | flops 1024 | bytes 7168 | tf_op jit(solution)/shard_map/pmax | solution.py:21
  229.4 4.9 exponential_reduce_fusion.1
  234.3 4.8 multiply_reduce_fusion
  239.1 69.6 %all-reduce.1 = (f32[512]{0:T(512)S(1)}, f32[512]{0:T(512)S(1)}) all-reduce(f32[512]{0:T(512)S(1)} %get-tuple-element.13, f32[512]{0:T(512)S(1)} %exponential_reduce_fusion.1), channel_id=1, replica_groups=mesh['dp'=2,'width'=4,'vocab'=32] {'vocab'}, use_global_device_ids=true, to_apply=%region_10.0 | all-reduce | flops 1024 | bytes 8192 | tf_op jit(solution)/shard_map/psum | solution.py:23
  308.7 5.9 %multiply_convert_fusion = bf16[512,2004]{0,1:T(8,128)(2,1)} fusion(f32[512,2004]{0,1:T(8,128)} %reshape.33, f32[512,2004]{0,1:T(8,128)} %all-reduce.6.cloned.1.call-done, f32[512]{0:T(512)S(1)} %get-tuple-element.21, f32[512]{0:T(512)S(1)} %get-tuple-element.20), kind=kLoop, calls=%fused_computation.2 | loop fusion | flops 5130240 | bytes 10264576 | tf_op jit(solution)/shard_map/convert_element_type | solution.py:36
  314.6 3.3 reshape.30
  317.9 9.5 %convolution_bitcast_fusion = f32[2,2048,1002]{1,2,0:T(8,128)} fusion(bf16[512,2,1002]{0,2,1:T(8,128)(2,1)} %reshape.30, bf16[512,2048]{1,0:T(8,128)(2,1)S(1)} %copy-done), kind=kOutput, calls=%fused_computation | convolution fusion | flops 4202692608 | bytes 20566016 | tf_op jit(solution)/shard_map/td,tkv->kdv/dot_general | solution.py:39
  327.4 17.9 %copy.14 = f32[2,2048,1002]{2,1,0:T(8,128)} copy(f32[2,2048,1002]{1,2,0:T(8,128)} %convolution_bitcast_fusion) | data formatting | bytes 32833536 | tf_op jit(solution)/shard_map/td,tkv->kdv/transpose | solution.py:39
  345.3 0.0 copy-start.2
  345.3 0.0 reduce-scatter.2.cloned.1.call-update
  345.4 1.6 copy-done.2
  346.9 9.5 %fusion.2 = f32[512,2048]{1,0:T(8,128)} fusion(bf16[512,2004]{0,1:T(8,128)(2,1)S(1)} %copy-done.2, bf16[2048,2004]{0,1:T(8,128)(2,1)} %reshape.29), kind=kOutput, calls=%fused_computation.11 | convolution fusion | flops 4202692608 | bytes 14454784 | tf_op jit(solution)/shard_map/dot_general | solution.py:44
  356.4 172.3 %all-reduce.7 = (f32[512]{0:T(512)S(1)}, bf16[512,2048]{1,0:T(8,128)(2,1)}) all-reduce(f32[512]{0:T(512)S(1)} %get-tuple-element.12, f32[512,2048]{1,0:T(8,128)} %fusion.2), channel_id=1, replica_groups=mesh['dp'=2,'width'=4,'vocab'=32] {'vocab'}, use_global_device_ids=true, to_apply=%region_4.0 | all-reduce | flops 1049088 | bytes 6295552 | tf_op jit(solution)/shard_map/psum | solution.py:23
  528.7 0.6 subtract_add_fusion
  529.3 0.0 reduce-scatter.2.cloned.1.call-done
  529.3 0.0 copy-start.1
  529.3 6.1 %convert_bitcast_fusion = bf16[2048,1,1002]{2,0,1:T(8,128)(2,1)} fusion(f32[2048,1002]{1,0:T(8,128)} %reduce-scatter.2.cloned.1.call-done), kind=kLoop, calls=%fused_computation.1 | loop fusion | flops 2052096 | bytes 12312576 | tf_op jit(solution)/shard_map/reshape | solution.py:43
  535.4 6.5 %copy.15 = bf16[2048,1,1002]{0,2,1:T(8,128)(2,1)} copy(bf16[2048,1,1002]{2,0,1:T(8,128)(2,1)} %convert_bitcast_fusion) | data formatting | bytes 8208384
  541.9 0.0 copy-done.1
  (1 shorter events, 0.0 us)
Async XLA Ops:
  7.2 38.7 %copy-start = (bf16[512,2048]{1,0:T(8,128)(2,1)S(1)}, bf16[512,2048]{1,0:T(8,128)(2,1)}, u32[]{:S(2)}) copy-start(bf16[512,2048]{1,0:T(8,128)(2,1)} %param.3) | copy-start | bytes 6291460
  7.2 30.6 %all-gather.2.cloned.1.call-start = ((), (), s32[]{:S(2)}) async-start(), calls=%async_computation.1 | async-start | bytes 12386304 | tf_op jit(solution)/shard_map/all_gather | solution.py:13
  7.9 143.7 %all-reduce.6.cloned.1.call-start = ((), (), s32[]{:S(2)}) async-start(), calls=%async_computation.2 | async-start | bytes 8224768 | tf_op jit(solution)/shard_map/psum | solution.py:17
  54.7 474.6 %reduce-scatter.2.cloned.1.call-start = ((), (), s32[]{:S(2)}) async-start(), calls=%async_computation.3 | async-start | bytes 25165824 | tf_op jit(solution)/shard_map/reduce_scatter | solution.py:40
  345.3 1.6 copy-start.2
  529.3 12.6 %copy-start.1 = (bf16[512,2048]{1,0:T(8,128)(2,1)S(1)}, bf16[512,2048]{1,0:T(8,128)(2,1)}, u32[]{:S(2)}) copy-start(bf16[512,2048]{1,0:T(8,128)(2,1)} %param.3) | copy-start | bytes 6291460
Sparse Core Ops, SparseCore 0:
  9.8 27.9 all-gather.1
  54.8 96.8 all-reduce.5
  345.5 27.6 reduce-scatter.1
where the time goes:
time: 549 us; the launch traced here: 548 us
  blocking collectives  317 us (58%)
  waiting for transfers between devices  115 us (21%)
  local copies, waits for them, and re-layouts  46 us (8%)
  other arithmetic  28.1 us (5%)
  matrix products  27.7 us (5%)
  between operations  13.8 us (3%)
    psum x2, blocking collectives, body(): lax.psum((jnp.sum(jnp.exp(student - student_peak[:, None]), axis=1), jnp....  242 us
    psum x1, waiting for transfers between devices, body(): student = lax.psum(partial_value, 'width')  84.9 us
    pmax x1, blocking collectives, body(): student_peak, target_peak = lax.pmax((student_peak, target_peak), 'vocab')  75.3 us
    all_gather x1, waiting for transfers between devices, body(): lax.all_gather(head, 'dp', axis=1, tiled=True)  29.8 us
    transpose x1, local copies, waits for them, and re-layouts, body(): jnp.einsum('td,tkv->kdv', hidden, grad_blocks, preferred_element_type=jnp...  17.9 us
  transfers between devices with their start and end apart: 3, of which 2 were waited for; matrix products, arithmetic and copies ran while one was open for 4% of the time, Pallas kernels for 0%

commit v1 on v0

--- a/solution.py
+++ b/solution.py
@@ -14,7 +14,8 @@
         width_cols, halves * local_cols
     )
     partial_value = jnp.dot(hidden, full_head, preferred_element_type=jnp.float32)
-    student = lax.psum(partial_value, "width")
+    terms = lax.all_gather(partial_value, "width")
+    student = jnp.sum(terms, axis=0)
     target = teacher.reshape(tok_rows, halves * local_cols).astype(jnp.float32)
     student_peak = jnp.max(student, axis=1)
     target_peak = jnp.max(target, axis=1)

time: 549 us -> 649 us (1.18)
  waiting for transfers between devices: 115 us -> 182 us
  other arithmetic: 28.1 us -> 43.5 us
  local copies, waits for them, and re-layouts: 46 us -> 58.7 us
    all_gather x0 -> x1, waiting for transfers between devices: none -> 152 us  [body(): terms = lax.all_gather(partial_value, 'width')]
    psum x1 -> x0, waiting for transfers between devices: 84.9 us -> none  [body(): student = lax.psum(partial_value, 'width')]
    reduce_sum x1 -> x2, other arithmetic: 4.76 us -> 27.7 us  [the longest x1 24.8 us: body(): student = jnp.sum(terms, axis=0)]
    all_gather x0 -> x1, local copies, waits for them, and re-layouts: none -> 20.1 us  [body(): terms = lax.all_gather(partial_value, 'width')]
    convert_element_type x2 -> x0, local copies, waits for them, and re-layouts: 8.68 us -> none  [body(): target = teacher.reshape(tok_rows, halves * local_cols).astype(jnp.float32)]
  transfers between devices with their start and end apart: 3 -> 3, of which waited for: 2 -> 2; matrix products, arithmetic and copies ran while one was open for 4% -> 2% of each run, Pallas kernels for 0% -> 0%
where the time goes in v1:
time: 649 us; the launch traced here: 647 us
  blocking collectives  317 us (49%)
  waiting for transfers between devices  182 us (28%)
  local copies, waits for them, and re-layouts  58.7 us (9%)
  other arithmetic  43.5 us (7%)
  matrix products  32.3 us (5%)
  between operations  13.8 us (2%)
    psum x2, blocking collectives, body(): lax.psum((jnp.sum(jnp.exp(student - student_peak[:, None]), axis=1), jnp....  241 us
    all_gather x1, waiting for transfers between devices, body(): terms = lax.all_gather(partial_value, 'width')  152 us
    pmax x1, blocking collectives, body(): student_peak, target_peak = lax.pmax((student_peak, target_peak), 'vocab')  75.3 us
    all_gather x1, waiting for transfers between devices, body(): lax.all_gather(head, 'dp', axis=1, tiled=True)  29.8 us
    reduce_sum x1, other arithmetic, body(): student = jnp.sum(terms, axis=0)  24.8 us
    all_gather x1, local copies, waits for them, and re-layouts, body(): terms = lax.all_gather(partial_value, 'width')  20.1 us
    transpose x1, local copies, waits for them, and re-layouts, body(): jnp.einsum('td,tkv->kdv', hidden, grad_blocks, preferred_element_type=jnp...  17.9 us
  transfers between devices with their start and end apart: 3, of which 2 were waited for; matrix products, arithmetic and copies ran while one was open for 2% of the time, Pallas kernels for 0%

profile of v1, /device:TPU:2, one launch (start us, length us, event | category | flops | bytes accessed | tf_op | source)
XLA Modules:
  0.0 647.4 jit_solution(9629284523927074222)
XLA Ops:
  7.2 0.0 copy-start
  7.2 0.0 all-gather.4.cloned.1.call-start
  7.2 0.7 all-gather.4.cloned.1.call-update
  7.9 0.0 all-gather.6.cloned.1.call-start
  8.0 29.8 %all-gather.4.cloned.1.call-done = bf16[2048,2,1002]{0,2,1:T(8,128)(2,1)} async-done(((bf16[2048,1,1002]{0,2,1:T(8,128)(2,1)}), bf16[2048,2,1002]{0,2,1:T(8,128)(2,1)}) %all-gather.4.cloned.1.call-update) | async-done | bytes 8208400 | tf_op jit(solution)/shard_map/all_gather | solution.py:13
  37.8 8.1 %reshape.52 = bf16[2048,2004]{0,1:T(8,128)(2,1)} reshape(bf16[2048,2,1002]{0,2,1:T(8,128)(2,1)} %all-gather.4.cloned.1.call-done) | data formatting | bytes 16416768 | tf_op jit(solution)/shard_map/reshape | solution.py:13
  45.9 0.0 copy-done
  45.9 8.9 %fusion.11 = f32[512,2004]{0,1:T(8,128)} fusion(bf16[512,2048]{1,0:T(8,128)(2,1)S(1)} %copy-done, bf16[2048,2004]{0,1:T(8,128)(2,1)} %reshape.52), kind=kOutput, calls=%fused_computation.19 | convolution fusion | flops 4202692608 | bytes 14409728 | tf_op jit(solution)/shard_map/dot_general | solution.py:16
  54.7 0.0 all-gather.6.cloned.1.call-update
  54.7 0.0 reduce-scatter.2.cloned.1.call-start
  54.8 3.3 reduce_max.23
  58.1 151.9 %all-gather.6.cloned.1.call-done = f32[2048,2004]{0,1:T(8,128)} async-done(((f32[512,2004]{0,1:T(8,128)}), f32[2048,2004]{0,1:T(8,128)}) %all-gather.6.cloned.1.call-update) | async-done | bytes 16416784 | tf_op jit(solution)/shard_map/all_gather | solution.py:17
  210.0 20.1 %reshape.55 = f32[4,512,2004]{1,0,2:T(4,128)} reshape(f32[2048,2004]{0,1:T(8,128)} %all-gather.6.cloned.1.call-done) | data formatting | bytes 32833536 | tf_op jit(solution)/shard_map/all_gather | solution.py:17
  230.1 24.8 %reduce_sum.38 = f32[512,2004]{0,1:T(8,128)} reduce(f32[4,512,2004]{1,0,2:T(4,128)} %reshape.55, f32[]{:T(128)} %constant.2.clone.1), dimensions={0}, to_apply=%region_2.0 | reduce | flops 3078144 | bytes 20520964 | tf_op jit(solution)/shard_map/reduce_sum | solution.py:18
  254.9 4.5 reduce_sum.39
  259.4 2.5 reduce_max.25
  261.9 75.3 %all-reduce.2 = (f32[512]{0:T(512)S(1)}, f32[512]{0:T(512)S(1)}) all-reduce(f32[512]{0:T(512)S(1)} %reduce_max.25, bf16[512]{0:T(512)(128)(2,1)S(1)} %reduce_max.23), channel_id=1, replica_groups=mesh['dp'=2,'width'=4,'vocab'=32] {'vocab'}, use_global_device_ids=true, to_apply=%region_8.0 | all-reduce | flops 1024 | bytes 7168 | tf_op jit(solution)/shard_map/pmax | solution.py:22
  337.2 0.0 copy-start.2
  337.2 2.9 exponential_reduce_fusion
  340.1 0.0 copy-done.2
  340.1 3.3 fusion.1
  343.4 69.7 %all-reduce.1 = (f32[512]{0:T(512)S(1)}, f32[512]{0:T(512)S(1)}) all-reduce(f32[512]{0:T(512)S(1)} %exponential_reduce_fusion, f32[512]{0:T(512)S(1)} %get-tuple-element.9), channel_id=1, replica_groups=mesh['dp'=2,'width'=4,'vocab'=32] {'vocab'}, use_global_device_ids=true, to_apply=%region_10.0 | all-reduce | flops 1024 | bytes 8192 | tf_op jit(solution)/shard_map/psum | solution.py:24
  413.1 11.3 %convolution_bitcast_fusion = f32[2,2048,1002]{1,2,0:T(8,128)} fusion(bf16[512,2048]{1,0:T(8,128)(2,1)S(1)} %copy-done, f32[512,2,1002]{0,2,1:T(8,128)} %reduce_sum.39, f32[512]{0:T(512)S(1)} %get-tuple-element.18, f32[512]{0:T(512)S(1)} %get-tuple-element.17, bf16[512,2,1002]{0,1,2:T(2,128)(2,1)} %param.5), kind=kOutput, calls=%fused_computation | convolution fusion | flops 4208848896 | bytes 24674304 | tf_op jit(solution)/shard_map/td,tkv->kdv/dot_general | solution.py:40
  424.4 17.9 %copy.12 = f32[2,2048,1002]{2,1,0:T(8,128)} copy(f32[2,2048,1002]{1,2,0:T(8,128)} %convolution_bitcast_fusion) | data formatting | bytes 32833536 | tf_op jit(solution)/shard_map/td,tkv->kdv/transpose | solution.py:40
  442.3 0.0 copy-start.3
  442.3 0.0 reduce-scatter.2.cloned.1.call-update
  442.3 1.5 copy-done.3
  443.9 12.2 %convolution_bitcast_fusion.1 = f32[512,2048]{1,0:T(8,128)} fusion(bf16[2048,2,1002]{0,2,1:T(8,128)(2,1)} %all-gather.4.cloned.1.call-done, f32[512,2,1002]{0,2,1:T(8,128)} %reduce_sum.39, f32[512]{0:T(512)S(1)} %get-tuple-element.18, f32[512]{0:T(512)S(1)} %get-tuple-element.17, bf16[512,2,1002]{0,1,2:T(2,128)(2,1)S(1)} %copy-done.3), kind=kOutput, calls=%fused_computation.14 | convolution fusion | flops 4208848896 | bytes 18563072 | tf_op jit(solution)/shard_map/dot_general | solution.py:45
  456.0 171.7 %all-reduce.4 = (f32[512]{0:T(512)S(1)}, bf16[512,2048]{1,0:T(8,128)(2,1)}) all-reduce(f32[512]{0:T(512)S(1)} %get-tuple-element.10, f32[512,2048]{1,0:T(8,128)} %convolution_bitcast_fusion.1), channel_id=1, replica_groups=mesh['dp'=2,'width'=4,'vocab'=32] {'vocab'}, use_global_device_ids=true, to_apply=%region_4.0 | all-reduce | flops 1049088 | bytes 6295552 | tf_op jit(solution)/shard_map/psum | solution.py:24
  627.7 0.6 subtract_add_fusion
  628.3 0.0 reduce-scatter.2.cloned.1.call-done
  628.3 0.0 copy-start.1
  628.3 6.1 convert_bitcast_fusion
  634.4 6.5 copy.13
  640.9 0.0 copy-done.1
  (1 shorter events, 0.0 us)
Async XLA Ops:
  7.2 38.7 %copy-start = (bf16[512,2048]{1,0:T(8,128)(2,1)S(1)}, bf16[512,2048]{1,0:T(8,128)(2,1)}, u32[]{:S(2)}) copy-start(bf16[512,2048]{1,0:T(8,128)(2,1)} %param.3) | copy-start | bytes 6291460
  7.2 30.6 %all-gather.4.cloned.1.call-start = ((), (), s32[]{:S(2)}) async-start(), calls=%async_computation.1 | async-start | bytes 12386304 | tf_op jit(solution)/shard_map/all_gather | solution.py:13
  7.9 202.1 %all-gather.6.cloned.1.call-start = ((), (), s32[]{:S(2)}) async-start(), calls=%async_computation.3 | async-start | bytes 20561920 | tf_op jit(solution)/shard_map/all_gather | solution.py:17
  54.7 573.6 %reduce-scatter.2.cloned.1.call-start = ((), (), s32[]{:S(2)}) async-start(), calls=%async_computation.2 | async-start | bytes 25165824 | tf_op jit(solution)/shard_map/reduce_scatter | solution.py:41
  337.2 2.9 copy-start.2
  442.3 1.6 copy-start.3
  628.3 12.6 %copy-start.1 = (bf16[512,2048]{1,0:T(8,128)(2,1)S(1)}, bf16[512,2048]{1,0:T(8,128)(2,1)}, u32[]{:S(2)}) copy-start(bf16[512,2048]{1,0:T(8,128)(2,1)} %param.3) | copy-start | bytes 6291460
Sparse Core Ops, SparseCore 0:
  9.8 27.9 all-gather.3
  54.8 155.0 all-gather.5
  442.4 27.6 reduce-scatter.1
